TPU v7x, 32 devices: a whole 2x2x4 slice. The times are simulated.
32 devices in a mesh: occ: 4 (over z), vir: 8 (over y, x, core).
Axes of the slice: x: 2, y: 2, z: 4, core: 2. Of those that a mesh axis runs over, the one named last changes fastest.
Arguments:
- amplitudes: bfloat16 [40, 40, 400, 400], P('occ', None, 'vir'), may hold values from -6 to 6
- integrals: bfloat16 [400, 400, 3200], P('vir', 'occ'), may hold values from -0.109375 to 0.109375
- batch_index: int32 [1], replicated, may hold values from 0 to 49
- eps_occ: float32 [40], replicated, may hold values from -1 to -0.3
- eps_vir: float32 [400], replicated, may hold values from 0.2 to 1.5
Outputs:
- update: float32 [400, 400, 1600], P(None, 'vir', 'occ')
Inputs may be any that keep to these rules, and one draw needn't show every extreme that they name: Selects the virtual orbitals d from 8 * batch_index to 8 * batch_index + 7.
All inputs are finite; a program needn't handle non-finite values.
Results may differ from a plain program's by a relative error of at most 0.0029.
Values may be sent and summed in bfloat16 or wider, within the bound.
A program may use at most 384 MiB of HBM per device.

v0:
```python
import jax
import jax.numpy as jnp
from jax import lax
from jax.sharding import PartitionSpec as P

NB = 8


def shards(amplitudes, integrals, batch_index, eps_occ, eps_vir):
    occ_rows = amplitudes.shape[0]
    occ_all = amplitudes.shape[1]
    vir_local = amplitudes.shape[2]
    block_a = integrals.shape[0]
    block_b = integrals.shape[1]
    begin = batch_index[0] * NB
    sliced = lax.dynamic_slice_in_dim(amplitudes, begin, NB, 3)
    sliced = sliced.reshape(occ_rows, occ_all, vir_local * NB)
    weights_flat = integrals.reshape(block_a * block_b, integrals.shape[2])
    dims_last = (((1,), (1,)), ((), ()))
    columns = lax.all_gather(sliced, "vir", axis=2, tiled=True)
    columns = columns.reshape(occ_rows * occ_all, columns.shape[2])
    ladder = lax.dot_general(
        weights_flat,
        lax.all_gather(columns, "occ", axis=0, tiled=True),
        dims_last,
        preferred_element_type=jnp.float32,
    )
    ladder = 0.5 * ladder.reshape(block_a, block_b, occ_all, occ_all)
    mixed = (ladder - jnp.transpose(ladder, (0, 1, 3, 2))).astype(jnp.bfloat16)
    mixed = mixed.reshape(block_a, block_b, occ_all * occ_all)
    relaid = lax.all_to_all(
        lax.all_to_all(mixed, "occ", split_axis=2, concat_axis=1, tiled=True),
        "vir",
        split_axis=1,
        concat_axis=0,
        tiled=True,
    )
    returned = lax.all_to_all(relaid, "vir", split_axis=0, concat_axis=1, tiled=True)
    mirrored = jnp.swapaxes(returned, 0, 1)
    pair_count = relaid.shape[2]
    pair_rows = pair_count // occ_all
    width_b = relaid.shape[1]
    occ_index = lax.axis_index("occ")
    vir_index = lax.axis_index("vir")
    energy_rows = lax.dynamic_slice_in_dim(eps_occ, occ_index * pair_rows, pair_rows, 0)
    pair_energy = (energy_rows[:, None] + eps_occ[None, :]).reshape(pair_count)
    energy_cols = lax.dynamic_slice_in_dim(eps_vir, vir_index * width_b, width_b, 0)
    denominator = pair_energy[None, None, :] - eps_vir[:, None, None] - energy_cols[None, :, None]
    return (relaid.astype(jnp.float32) - mirrored.astype(jnp.float32)) / denominator


def solution(mesh):
    in_specs = (P("occ", None, "vir", None), P("vir", "occ", None), P(), P(), P())
    out_specs = P(None, "vir", "occ")
    return jax.shard_map(shards, mesh=mesh, in_specs=in_specs, out_specs=out_specs, check_vma=False)
```

profile of v0, /device:TPU:0, one launch (start us, length us, event | category | flops | bytes accessed | tf_op | source)
XLA Modules:
  0.0 1750.7 jit_solution(14106090877960667524)
XLA Ops:
  7.2 6.2 constant_dynamic-slice_fusion
  13.4 4.9 copy.30
  18.4 56.2 %all-gather.3.cloned.1.call-done = bf16[10,40,3200]{1,2,0:T(8,128)(2,1)} async-done(((bf16[10,40,400]{1,2,0:T(8,128)(2,1)}), bf16[10,40,3200]{1,2,0:T(8,128)(2,1)}) %all-gather.3.cloned.1.call-update) | async-done | bytes 2560016 | tf_op jit(solution)/shard_map/all_gather | solution.py:20
  74.6 8.3 copy.31
  82.9 33.5 %reshape.69 = bf16[5000,3200]{1,0:T(8,128)(2,1)} reshape(bf16[50,100,3200]{2,1,0:T(8,128)(2,1)} %param.6) | data formatting | bytes 64000000 | tf_op jit(solution)/shard_map/reshape | solution.py:18
  116.4 146.5 %all-gather.5.cloned.1.call-done = bf16[1600,3200]{1,0:T(8,128)(2,1)} async-done(((bf16[400,3200]{1,0:T(8,128)(2,1)}), bf16[1600,3200]{1,0:T(8,128)(2,1)}) %all-gather.5.cloned.1.call-update) | async-done | bytes 10240016 | tf_op jit(solution)/shard_map/all_gather | solution.py:24
  263.0 65.0 %multiply_bitcast_fusion = f32[5000,1600]{0,1:T(8,128)} fusion(bf16[1600,3200]{1,0:T(8,128)(2,1)} %all-gather.5.cloned.1.call-done, bf16[5000,3200]{1,0:T(8,128)(2,1)} %reshape.69), kind=kOutput, calls=%fused_computation.4 | convolution fusion | flops 51207999488 | bytes 74240000 | tf_op jit(solution)/shard_map/dot_general | solution.py:22
  327.9 43.7 %mul.29 = f32[50,100,40,40]{1,0,3,2:T(8,128)} reshape(f32[5000,1600]{0,1:T(8,128)} %multiply_bitcast_fusion) | data formatting | bytes 64000000 | tf_op jit(solution)/shard_map/mul | solution.py:28
  371.7 36.6 %fusion = bf16[50,100,40,40]{1,0,3,2:T(8,128)(2,1)} fusion(f32[50,100,40,40]{1,0,3,2:T(8,128)} %mul.29), kind=kLoop, calls=%fused_computation.1 | loop fusion | flops 16000000 | bytes 48000000 | tf_op jit(solution)/shard_map/convert_element_type | solution.py:29
  408.3 509.0 %all_to_all.45 = bf16[50,100,1600]{1,0,2:T(8,128)(2,1)} all-to-all(bf16[50,100,1600]{1,0,2:T(8,128)(2,1)} %bitcast.31), channel_id=1, replica_groups=mesh['occ'=4,'vir'=8] {'occ'}, dimensions={2} | all-to-all | bytes 32000000 | tf_op jit(solution)/shard_map/all_to_all | solution.py:32
  917.3 35.0 %copy.41 = bf16[50,100,4,400]{3,2,1,0:T(4,128)(2,1)} copy(bf16[50,100,4,400]{1,0,3,2:T(8,128)(2,1)} %bitcast.32) | data formatting | bytes 32000000 | tf_op jit(solution)/shard_map/all_to_all | solution.py:32
  952.3 15.0 copy.42
  967.3 253.9 %all_to_all.46 = bf16[50,400,400]{2,0,1:T(8,128)(2,1)} all-to-all(bf16[50,400,400]{2,0,1:T(8,128)(2,1)S(1)} %bitcast.33), channel_id=1, replica_groups=mesh['occ'=4,'vir'=8] {'vir'}, dimensions={1} | all-to-all | bytes 32000000 | tf_op jit(solution)/shard_map/all_to_all | solution.py:31
  1221.2 16.3 copy.37
  1237.5 29.7 %all_to_all.40 = bf16[400,50,400]{2,0,1:T(8,128)(2,1)} reshape(bf16[8,50,50,400]{3,1,0,2:T(8,128)(2,1)} %copy.37) | data formatting | bytes 32000000 | tf_op jit(solution)/shard_map/all_to_all | solution.py:31
  1267.2 30.0 %copy.38 = bf16[400,50,400]{2,1,0:T(8,128)(2,1)} copy(bf16[400,50,400]{2,0,1:T(8,128)(2,1)} %all_to_all.40) | data formatting | bytes 32000000 | tf_op jit(solution)/shard_map/all_to_all | solution.py:31
  1297.2 6.6 all-to-all-start.2
  1304.1 0.1 broadcast_subtract_fusion
  1304.3 249.2 %all-to-all-done.2 = bf16[400,50,400]{2,1,0:T(8,128)(2,1)} async-done(((bf16[400,50,400]{2,1,0:T(8,128)(2,1)}), bf16[400,50,400]{2,1,0:T(8,128)(2,1)}, u32[]{:S(2)}, u32[]{:S(2)}) %all-to-all-start.2) | async-done | bytes 16000032 | tf_op jit(solution)/shard_map/all_to_all | solution.py:38
  1553.5 24.7 %copy_convert_fusion = f32[400,50,400]{2,0,1:T(8,128)} fusion(bf16[400,50,400]{2,1,0:T(8,128)(2,1)} %all-to-all-done.2), kind=kLoop, calls=%fused_computation.5 | loop fusion | flops 8000000 | bytes 48000000 | tf_op jit(solution)/shard_map/convert_element_type | solution.py:49
  1578.2 41.8 %reshape.72 = f32[8,50,50,400]{3,1,0,2:T(8,128)} reshape(f32[400,50,400]{2,0,1:T(8,128)} %copy_convert_fusion) | data formatting | bytes 64000000 | tf_op jit(solution)/shard_map/convert_element_type | solution.py:49
  1620.0 48.8 %copy.40 = f32[50,8,50,400]{3,2,1,0:T(8,128)} copy(f32[50,8,50,400]{3,0,1,2:T(8,128)} %bitcast.30) | data formatting | bytes 64000000 | tf_op jit(solution)/shard_map/convert_element_type | solution.py:49
  1668.8 41.8 %reshape.71 = f32[50,400,400]{2,1,0:T(8,128)} reshape(f32[50,8,50,400]{3,2,1,0:T(8,128)} %copy.40) | data formatting | bytes 64000000 | tf_op jit(solution)/shard_map/convert_element_type | solution.py:49
  1710.6 33.2 %fusion.1 = f32[400,50,400]{2,0,1:T(8,128)} fusion(f32[50,400,400]{2,1,0:T(8,128)} %reshape.71, bf16[400,50,400]{2,0,1:T(8,128)(2,1)} %all_to_all.40, f32[50]{0:T(128)S(1)} %dynamic_slice.11, f32[400,400]{1,0:T(8,128)S(1)} %broadcast_subtract_fusion), kind=kLoop, calls=%fused_computation.3 | loop fusion | flops 32000000 | bytes 80640200 | tf_op jit(solution)/shard_map/div | solution.py:49
  (12 shorter events, 0.4 us)
Async XLA Ops:
  6.5 68.1 %all-gather.3.cloned.1.call-start = ((), (), s32[]{:S(2)}) async-start(), calls=%async_computation.3 | async-start | bytes 9216000 | tf_op jit(solution)/shard_map/all_gather | solution.py:20
  18.3 244.6 %all-gather.5.cloned.1.call-start = ((), (), s32[]{:S(2)}) async-start(), calls=%async_computation.4 | async-start | bytes 12800000 | tf_op jit(solution)/shard_map/all_gather | solution.py:24
  1297.2 6.6 copy-start.1
  1297.2 6.9 copy-start
  1297.2 256.3 %all-to-all-start.2 = ((bf16[400,50,400]{2,1,0:T(8,128)(2,1)}), bf16[400,50,400]{2,1,0:T(8,128)(2,1)}, u32[]{:S(2)}, u32[]{:S(2)}) async-start(bf16[400,50,400]{2,1,0:T(8,128)(2,1)} %copy.38), calls=%async_computation.2 | async-start | bytes 45875200 | tf_op jit(solution)/shard_map/all_to_all | solution.py:38
Sparse Core Ops, SparseCore 0:
  18.5 56.1 all-gather.2
  83.1 179.8 all-gather.4
where the time goes:
time: 1760 us; the launch traced here: 1750 us
  blocking collectives  763 us (43%)
  waiting for transfers between devices  452 us (26%)
  local copies, waits for them, and re-layouts  355 us (20%)
  other arithmetic  94.7 us (5%)
  matrix products  65 us (4%)
    all_to_all x1, blocking collectives, shards(): lax.all_to_all(mixed, 'occ', split_axis=2, concat_axis=1, tiled=True)  509 us
    all_to_all x1, blocking collectives, shards(): lax.all_to_all(lax.all_to_all(mixed, 'occ', split_axis=2, concat_axis=1,...  254 us
    all_to_all x1, waiting for transfers between devices, shards(): lax.all_to_all(relaid, 'vir', split_axis=0, concat_axis=1, tiled=True)  249 us
    all_gather x1, waiting for transfers between devices, shards(): lax.all_gather(columns, 'occ', axis=0, tiled=True)  147 us
    convert_element_type x3, local copies, waits for them, and re-layouts, shards(): mirrored.astype(jnp.float32)  132 us
    all_to_all x3, local copies, waits for them, and re-layouts, shards(): lax.all_to_all(lax.all_to_all(mixed, 'occ', split_axis=2, concat_axis=1,...  76 us
    dot_general x1, matrix products, shards(): lax.dot_general(weights_flat, lax.all_gather(columns, 'occ', axis=0, tile...  65 us
    all_gather x1, waiting for transfers between devices, shards(): columns = lax.all_gather(sliced, 'vir', axis=2, tiled=True)  56.2 us
  transfers between devices with their start and end apart: 3, of which 3 were waited for; matrix products, arithmetic and copies ran while one was open for 2% of the time, Pallas kernels for 0%

commit v1 on v0

--- a/solution.py
+++ b/solution.py
@@ -28,12 +28,20 @@
     ladder = 0.5 * ladder.reshape(block_a, block_b, occ_all, occ_all)
     mixed = (ladder - jnp.transpose(ladder, (0, 1, 3, 2))).astype(jnp.bfloat16)
     mixed = mixed.reshape(block_a, block_b, occ_all * occ_all)
-    relaid = lax.all_to_all(
-        lax.all_to_all(mixed, "occ", split_axis=2, concat_axis=1, tiled=True),
-        "vir",
-        split_axis=1,
-        concat_axis=0,
-        tiled=True,
+    relaid = jnp.concatenate(
+        lax.all_to_all(
+            jnp.stack(
+                jnp.split(
+                    lax.all_to_all(mixed, "occ", split_axis=2, concat_axis=1, tiled=True),
+                    lax.axis_size("vir"),
+                    axis=1,
+                )
+            ),
+            "vir",
+            0,
+            0,
+        ),
+        axis=0,
     )
     returned = lax.all_to_all(relaid, "vir", split_axis=0, concat_axis=1, tiled=True)
     mirrored = jnp.swapaxes(returned, 0, 1)

time: 1760 us -> 1770 us (level)
    all_to_all x3 -> x1, local copies, waits for them, and re-layouts: 76 us -> 7.94 us  [shards(): lax.all_to_all(jnp.stack(jnp.split(lax.all_to_all(mixed, 'occ', split_axi...]
    reshape x0 -> x2, local copies, waits for them, and re-layouts: none -> 59.7 us  [shards(): jnp.concatenate(lax.all_to_all(jnp.stack(jnp.split(lax.all_to_all(mixed,...]
    unnamed x4 -> x13, local copies, waits for them, and re-layouts: 0.01 us -> 21.4 us
    all_to_all x2 -> x1, local copies, waits for them, and re-layouts: 50 us -> 47.2 us  [shards(): lax.all_to_all(mixed, 'occ', split_axis=2, concat_axis=1, tiled=True)]
where the time goes in v1:
time: 1770 us; the launch traced here: 1760 us
  blocking collectives  763 us (43%)
  waiting for transfers between devices  452 us (26%)
  local copies, waits for them, and re-layouts  367 us (21%)
  other arithmetic  94.7 us (5%)
  matrix products  65 us (4%)
    all_to_all x1, blocking collectives, shards(): lax.all_to_all(mixed, 'occ', split_axis=2, concat_axis=1, tiled=True)  509 us
    all_to_all x1, blocking collectives, shards(): lax.all_to_all(jnp.stack(jnp.split(lax.all_to_all(mixed, 'occ', split_axi...  254 us
    all_to_all x1, waiting for transfers between devices, shards(): lax.all_to_all(relaid, 'vir', split_axis=0, concat_axis=1, tiled=True)  249 us
    all_gather x1, waiting for transfers between devices, shards(): lax.all_gather(columns, 'occ', axis=0, tiled=True)  147 us
    convert_element_type x3, local copies, waits for them, and re-layouts, shards(): mirrored.astype(jnp.float32)  132 us
    dot_general x1, matrix products, shards(): lax.dot_general(weights_flat, lax.all_gather(columns, 'occ', axis=0, tile...  65 us
    reshape x2, local copies, waits for them, and re-layouts, shards(): jnp.concatenate(lax.all_to_all(jnp.stack(jnp.split(lax.all_to_all(mixed,...  59.7 us
    all_gather x1, waiting for transfers between devices, shards(): columns = lax.all_gather(sliced, 'vir', axis=2, tiled=True)  56.2 us
  transfers between devices with their start and end apart: 3, of which 3 were waited for; matrix products, arithmetic and copies ran while one was open for 2% of the time, Pallas kernels for 0%

profile of v1, /device:TPU:0, one launch (start us, length us, event | category | flops | bytes accessed | tf_op | source)
XLA Modules:
  0.0 1763.0 jit_solution(8494516812321461109)
XLA Ops:
  7.2 6.2 constant_dynamic-slice_fusion
  13.4 4.9 copy.47
  18.4 56.2 %all-gather.3.cloned.1.call-done = bf16[10,40,3200]{1,2,0:T(8,128)(2,1)} async-done(((bf16[10,40,400]{1,2,0:T(8,128)(2,1)}), bf16[10,40,3200]{1,2,0:T(8,128)(2,1)}) %all-gather.3.cloned.1.call-update) | async-done | bytes 2560016 | tf_op jit(solution)/shard_map/all_gather | solution.py:20
  74.6 8.3 copy.48
  82.9 33.5 %reshape.72 = bf16[5000,3200]{1,0:T(8,128)(2,1)} reshape(bf16[50,100,3200]{2,1,0:T(8,128)(2,1)} %param.6) | data formatting | bytes 64000000 | tf_op jit(solution)/shard_map/reshape | solution.py:18
  116.4 146.5 %all-gather.5.cloned.1.call-done = bf16[1600,3200]{1,0:T(8,128)(2,1)} async-done(((bf16[400,3200]{1,0:T(8,128)(2,1)}), bf16[1600,3200]{1,0:T(8,128)(2,1)}) %all-gather.5.cloned.1.call-update) | async-done | bytes 10240016 | tf_op jit(solution)/shard_map/all_gather | solution.py:24
  263.0 65.0 %multiply_bitcast_fusion = f32[5000,1600]{0,1:T(8,128)} fusion(bf16[1600,3200]{1,0:T(8,128)(2,1)} %all-gather.5.cloned.1.call-done, bf16[5000,3200]{1,0:T(8,128)(2,1)} %reshape.72), kind=kOutput, calls=%fused_computation.4 | convolution fusion | flops 51207999488 | bytes 74240000 | tf_op jit(solution)/shard_map/dot_general | solution.py:22
  327.9 43.7 %mul.29 = f32[50,100,40,40]{1,0,3,2:T(8,128)} reshape(f32[5000,1600]{0,1:T(8,128)} %multiply_bitcast_fusion) | data formatting | bytes 64000000 | tf_op jit(solution)/shard_map/mul | solution.py:28
  371.6 36.6 %fusion = bf16[50,100,40,40]{1,0,3,2:T(8,128)(2,1)} fusion(f32[50,100,40,40]{1,0,3,2:T(8,128)} %mul.29), kind=kLoop, calls=%fused_computation.1 | loop fusion | flops 16000000 | bytes 48000000 | tf_op jit(solution)/shard_map/convert_element_type | solution.py:29
  408.3 509.0 %all_to_all.32 = bf16[50,100,1600]{1,0,2:T(8,128)(2,1)} all-to-all(bf16[50,100,1600]{1,0,2:T(8,128)(2,1)} %bitcast.60), channel_id=1, replica_groups=mesh['occ'=4,'vir'=8] {'occ'}, dimensions={2} | all-to-all | bytes 32000000 | tf_op jit(solution)/shard_map/all_to_all | solution.py:35
  917.3 47.2 %copy.50 = bf16[50,100,4,400]{3,0,1,2:T(8,128)(2,1)} copy(bf16[50,100,4,400]{1,0,3,2:T(8,128)(2,1)} %bitcast.61) | data formatting | bytes 32000000 | tf_op jit(solution)/shard_map/all_to_all | solution.py:35
  968.2 4.4 fusion.8
  972.5 4.4 fusion.7
  987.6 254.2 %all_to_all.33 = bf16[8,50,50,400]{3,1,2,0:T(8,128)(2,1)S(1)} all-to-all(bf16[8,50,50,400]{3,1,2,0:T(8,128)(2,1)} %fusion.2), channel_id=1, replica_groups=mesh['occ'=4,'vir'=8] {'vir'}, dimensions={0} | all-to-all | bytes 32000000 | tf_op jit(solution)/shard_map/all_to_all | solution.py:32
  1241.9 7.9 copy.51
  1249.8 29.7 %reshape.74 = bf16[400,50,400]{2,0,1:T(8,128)(2,1)} reshape(bf16[8,50,50,400]{3,1,0,2:T(8,128)(2,1)} %copy.51) | data formatting | bytes 32000000 | tf_op jit(solution)/shard_map/reshape | solution.py:31
  1279.5 30.0 %copy.52 = bf16[400,50,400]{2,1,0:T(8,128)(2,1)} copy(bf16[400,50,400]{2,0,1:T(8,128)(2,1)} %reshape.74) | data formatting | bytes 32000000 | tf_op jit(solution)/shard_map/reshape | solution.py:31
  1309.5 6.6 all-to-all-start.2
  1316.6 249.2 %all-to-all-done.2 = bf16[400,50,400]{2,1,0:T(8,128)(2,1)} async-done(((bf16[400,50,400]{2,1,0:T(8,128)(2,1)}), bf16[400,50,400]{2,1,0:T(8,128)(2,1)}, u32[]{:S(2)}, u32[]{:S(2)}) %all-to-all-start.2) | async-done | bytes 16000032 | tf_op jit(solution)/shard_map/all_to_all | solution.py:46
  1565.8 24.7 %copy_convert_fusion = f32[400,50,400]{2,0,1:T(8,128)} fusion(bf16[400,50,400]{2,1,0:T(8,128)(2,1)} %all-to-all-done.2), kind=kLoop, calls=%fused_computation.5 | loop fusion | flops 8000000 | bytes 48000000 | tf_op jit(solution)/shard_map/convert_element_type | solution.py:57
  1590.5 41.8 %reshape.76 = f32[8,50,50,400]{3,1,0,2:T(8,128)} reshape(f32[400,50,400]{2,0,1:T(8,128)} %copy_convert_fusion) | data formatting | bytes 64000000 | tf_op jit(solution)/shard_map/convert_element_type | solution.py:57
  1632.3 48.8 %copy.54 = f32[50,8,50,400]{3,2,1,0:T(8,128)} copy(f32[50,8,50,400]{3,0,1,2:T(8,128)} %bitcast.59) | data formatting | bytes 64000000 | tf_op jit(solution)/shard_map/convert_element_type | solution.py:57
  1681.1 41.8 %reshape.75 = f32[50,400,400]{2,1,0:T(8,128)} reshape(f32[50,8,50,400]{3,2,1,0:T(8,128)} %copy.54) | data formatting | bytes 64000000 | tf_op jit(solution)/shard_map/convert_element_type | solution.py:57
  1722.9 33.2 %fusion.1 = f32[400,50,400]{2,0,1:T(8,128)} fusion(f32[50,400,400]{2,1,0:T(8,128)} %reshape.75, bf16[400,50,400]{2,0,1:T(8,128)(2,1)} %reshape.74, f32[50]{0:T(128)S(1)} %dynamic_slice.11, f32[400,400]{1,0:T(8,128)S(1)} %broadcast_subtract_fusion), kind=kLoop, calls=%fused_computation.3 | loop fusion | flops 32000000 | bytes 80640200 | tf_op jit(solution)/shard_map/div | solution.py:57
  (21 shorter events, 15.0 us)
Async XLA Ops:
  6.5 68.1 %all-gather.3.cloned.1.call-start = ((), (), s32[]{:S(2)}) async-start(), calls=%async_computation.3 | async-start | bytes 9216000 | tf_op jit(solution)/shard_map/all_gather | solution.py:20
  18.3 244.6 %all-gather.5.cloned.1.call-start = ((), (), s32[]{:S(2)}) async-start(), calls=%async_computation.4 | async-start | bytes 12800000 | tf_op jit(solution)/shard_map/all_gather | solution.py:24
  964.5 16.1 copy-start
  1309.5 6.6 copy-start.2
  1309.5 6.9 copy-start.1
  1309.5 256.3 %all-to-all-start.2 = ((bf16[400,50,400]{2,1,0:T(8,128)(2,1)}), bf16[400,50,400]{2,1,0:T(8,128)(2,1)}, u32[]{:S(2)}, u32[]{:S(2)}) async-start(bf16[400,50,400]{2,1,0:T(8,128)(2,1)} %copy.52), calls=%async_computation.2 | async-start | bytes 45875200 | tf_op jit(solution)/shard_map/all_to_all | solution.py:46
Sparse Core Ops, SparseCore 0:
  18.5 56.1 all-gather.2
  83.0 179.8 all-gather.4
